TPU v7x, 256 devices: a whole 4x4x8 slice. The times are simulated.
256 devices in a mesh: band: 8 (over y, core), plane: 32 (over x, z).
Axes of the slice: x: 4, y: 4, z: 8, core: 2. Of those that a mesh axis runs over, the one named last changes fastest.
Arguments:
- psi: float32 [2, 8, 4096, 128], P(None, 'band', 'plane'), may hold values from -8 to 8
- potential: float32 [96, 9216], P('plane'), may hold values from 0 to 2
- stick_column: int32 [4096], P('plane'), may hold values from 0 to 9215, as said below
- stick_length: int32 [4096], P('plane'), may hold values from 0 to 49, as said below
Outputs:
- psi_new: float32 [2, 8, 4096, 128], P(None, 'band', 'plane')
- potential_new: float32 [96, 9216], P('plane')
Inputs may be any that keep to these rules, and one draw needn't show every extreme that they name: `stick_column`: within each device's block of 128 slots the live sticks come first and the other slots are empty with column 0. Over all devices the live slots hold every column (mx mod 96) * 96 + (my mod 96) with mx * mx + my * my <= 576 exactly once, in an order drawn from the seed; some device's block is full and the others hold fewer. `stick_length`: A live slot's length is 2 h + 1, with h the largest whole number such that mx * mx + my * my + h * h <= 576 for its column; empty slots have length 0.
All inputs are finite; a program needn't handle non-finite values.
Results may differ from a plain program's by a relative error of at most 0.0001.
Values sent between devices are 32-bit elements; how exact they have to be, the bound alone decides.
No kernel may reach another device: no remote copies, remote signals or barrier semaphores. Data moves between devices by JAX's collectives and lax.ppermute only.
A program may use at most 64 MiB of HBM per device.

v0:
```python
import math
import jax
import jax.numpy as jnp
from jax import lax
from jax.sharding import PartitionSpec as P

NG = 96
RAD = 24
STICK_COEFFS = 128
BAND_DEV = 1
HIGHEST = lax.Precision.HIGHEST
TIMESTEP = 0.6
LINEAR_GAIN = 0.5
CUBIC_GAIN = 0.3


def turning(values):
    return values.astype(jnp.float32) * (2.0 * math.pi / NG)


def height_tables(lengths, columns, planes, device_list):
    order = jnp.arange(STICK_COEFFS, dtype=jnp.int32)
    height = (
        jnp.arange(device_list, dtype=jnp.int32)[None, :] * planes
        + jnp.arange(planes, dtype=jnp.int32)[:, None]
    )
    scale = NG ** (-0.5)
    wave_angle = turning(order[:, None, None] * height[None, :, :] % NG)
    wave = (jnp.cos(wave_angle) * scale, jnp.sin(wave_angle) * scale)
    half = (lengths - 1) // 2
    shift_angle = -turning(height[:, :, None] * half[None, None, :] % NG)
    shift = (jnp.cos(shift_angle), jnp.sin(shift_angle))
    mask = (order[None, :] < lengths[:, None]).astype(jnp.float32)
    first = columns // NG
    second = columns % NG
    first = jnp.where(first > NG // 2, first - NG, first)
    second = jnp.where(second > NG // 2, second - NG, second)
    depth = order[None, :] - half[:, None]
    kinetic = (
        ((first * first + second * second)[:, None] + depth * depth).astype(jnp.float32)
        / (RAD * RAD)
        * mask
    )
    return (wave, shift, mask, kinetic)


def along_height(terms, tables):
    wave, shift = (tables[0], tables[1])

    def contract(left, right):
        return jnp.einsum("bsj,jdn->bdns", left, right, precision=HIGHEST)

    upper_real = contract(terms[0], wave[0]) - contract(terms[1], wave[1])
    upper_imag = contract(terms[0], wave[1]) + contract(terms[1], wave[0])
    return jnp.stack(
        [
            upper_real * shift[0] - upper_imag * shift[1],
            upper_real * shift[1] + upper_imag * shift[0],
        ]
    )


def from_height(values, tables):
    wave, shift, mask = (tables[0], tables[1], tables[2])
    turned_real = values[0] * shift[0] + values[1] * shift[1]
    turned_imag = values[1] * shift[0] - values[0] * shift[1]

    def contract(left, right):
        return jnp.einsum("bdns,jdn->bsj", left, right, precision=HIGHEST)

    real_part = contract(turned_real, wave[0]) + contract(turned_imag, wave[1])
    imag_part = contract(turned_imag, wave[0]) - contract(turned_real, wave[1])
    return jnp.stack([real_part * mask, imag_part * mask])


def plane_tables():
    index = jnp.arange(NG, dtype=jnp.int32)
    angle = turning(index[:, None] * index[None, :] % NG)
    scale = NG ** (-0.5)
    return (jnp.cos(angle) * scale, jnp.sin(angle) * scale)


def plane_transform(values, cosine, sine):
    bands, planes = (values.shape[1], values.shape[2])
    real_part = values[0].reshape(bands, planes, NG, NG)
    imag_part = values[1].reshape(bands, planes, NG, NG)

    def inner(left, right):
        return jnp.einsum("bdmk,ky->bdmy", left, right, precision=HIGHEST)

    def outer(left, right):
        return jnp.einsum("mx,bdmy->bdxy", left, right, precision=HIGHEST)

    middle_real = inner(real_part, cosine) - inner(imag_part, sine)
    middle_imag = inner(real_part, sine) + inner(imag_part, cosine)
    final_real = outer(cosine, middle_real) - outer(sine, middle_imag)
    final_imag = outer(sine, middle_real) + outer(cosine, middle_imag)
    return jnp.stack([final_real, final_imag]).reshape(2, bands, planes, NG * NG)


def cell_slots(columns, lengths):
    count = columns.shape[0]
    target = jnp.where(lengths > 0, columns, NG * NG)
    table = jnp.full((NG * NG,), -1, jnp.int32)
    return table.at[target].set(jnp.arange(count, dtype=jnp.int32), mode="drop")


def spread_columns(values, table):
    picked = jnp.take(values, jnp.maximum(table, 0), axis=3)
    return jnp.where(table >= 0, picked, 0.0)


def modulus(field):
    return jnp.sum(field[0] * field[0] + field[1] * field[1], axis=0)


def advance(applied, power):
    factor = TIMESTEP / power
    return jnp.stack([factor * applied[1], -factor * applied[0]])


def shards(psi, potential, stick_column, stick_length):
    device_list = lax.axis_size("plane")
    planes = potential.shape[0]
    slots = stick_column.shape[0]
    bands = psi.shape[1]
    cosine, sine = plane_tables()
    own = height_tables(stick_length, stick_column, planes, device_list)
    term = psi * own[2]
    columns, lengths = (
        lax.all_gather(stick_column, "plane", axis=0, tiled=True),
        lax.all_gather(stick_length, "plane", axis=0, tiled=True),
    )
    given_cells = cell_slots(columns, lengths)
    total = term
    before = jnp.zeros((planes, NG * NG), jnp.float32)
    for power in range(1, 4):
        arrived = lax.all_to_all(
            along_height(term, own), "plane", split_axis=3, concat_axis=3, tiled=True
        ).reshape(2, bands, planes, device_list * slots)
        field = plane_transform(spread_columns(arrived, given_cells), cosine, sine)
        if power == 1:
            before = modulus(field)
        spectrum = plane_transform(field * potential, cosine, -sine)
        picked = spectrum[:, :, :, columns].reshape(2, bands, planes, device_list, slots)
        returned = lax.all_to_all(picked, "plane", split_axis=3, concat_axis=3, tiled=True)
        term = advance(from_height(returned, own) + own[3] * term, power)
        total = total + term
    arrived = lax.all_to_all(
        along_height(total, own), "plane", split_axis=3, concat_axis=3, tiled=True
    ).reshape(2, bands, planes, device_list * slots)
    after = modulus(plane_transform(spread_columns(arrived, given_cells), cosine, sine))
    change = (after - before) / BAND_DEV
    whole = lax.psum(change, "band")
    potential_new = potential + LINEAR_GAIN * whole + CUBIC_GAIN * whole * whole * whole
    return (total, potential_new)


def solution(mesh):
    in_specs = (P(None, "band", "plane", None), P("plane", None), P("plane"), P("plane"))
    out_specs = (P(None, "band", "plane", None), P("plane", None))
    return jax.shard_map(shards, mesh=mesh, in_specs=in_specs, out_specs=out_specs, check_vma=False)
```

profile of v0, /device:TPU:2, one launch (start us, length us, event | category | flops | bytes accessed | tf_op | source)
XLA Modules:
  0.0 968.3 jit_solution(16766717710354045417)
XLA Ops:
  12.2 11.6 %all-to-all-start = ((f32[2,1,3,32,128]{4,0,2,1,3:T(2,128)}), f32[2,1,3,32,128]{4,0,2,1,3:T(2,128)S(1)}, u32[]{:S(2)}, u32[]{:S(2)}) async-start(f32[2,1,3,32,128]{4,0,2,1,3:T(2,128)} %copy.177), calls=%async_computation | async-start | bytes 196608 | tf_op jit(solution)/shard_map/all_to_all | solution.py:138
  23.8 39.6 %all-gather = s32[32,1,128]{2,1,0:T(1,128)S(1)} all-gather(s32[1,1,128]{2,1,0:T(1,128)} %bitcast.566), channel_id=1, replica_groups=mesh['band'=8,'plane'=32] {'plane'}, dimensions={0}, use_global_device_ids=true | all-gather | bytes 16896 | tf_op jit(solution)/shard_map/all_gather | solution.py:132
  63.4 36.7 %all-gather.1 = s32[32,1,128]{2,1,0:T(1,128)S(1)} all-gather(s32[1,1,128]{2,1,0:T(1,128)} %bitcast.567), channel_id=1, replica_groups=mesh['band'=8,'plane'=32] {'plane'}, dimensions={0}, use_global_device_ids=true | all-gather | bytes 16896 | tf_op jit(solution)/shard_map/all_gather | solution.py:131
  100.1 15.5 %scatter_custom_fusion = s32[9216]{0:T(1024)S(1)} fusion(s32[4096]{0:T(1024)S(1)} %get-tuple-element.40, s32[4096]{0:T(1024)S(1)} %iota.105, s32[]{:T(128)} %constant.56.clone.1), kind=kCustom, calls=%fused_computation.291 | custom fusion | bytes 36868 | tf_op jit(solution)/shard_map/scatter | solution.py:105
  116.4 4.3 copy.179
  120.7 65.0 %gather_fusion.3 = f32[9216,2,3]{2,1,0:T(2,128)} fusion(f32[2,3,4096]{1,0,2:T(2,128)} %bitcast.554, s32[9216]{0:T(1024)S(1)} %maximum_clamp_fusion), kind=kCustom, calls=%fused_computation.clone | custom fusion | bytes 479232 | tf_op jit(solution)/shard_map/jit(_take)/gather | solution.py:109
  185.7 42.6 %fusion.3 = f32[2,1,3,9216]{2,0,3,1:T(2,128)S(1)} fusion(f32[9216,2,3]{2,1,0:T(2,128)} %gather_fusion.3, pred[9216]{0:T(1024)(128)(4,1)S(1)} %get-tuple-element.38, pred[9216]{0:T(1024)(128)(4,1)S(1)} %get-tuple-element.37), kind=kLoop, calls=%fused_computation.15 | loop fusion | flops 110592 | bytes 460800 | tf_op jit(solution)/shard_map/jit(_where)/select_n | solution.py:110
  228.3 8.5 fusion.517
  236.8 3.1 copy.281
  240.9 3.6 copy.282
  254.3 8.9 copy.194
  263.2 31.8 %gather_fusion = f32[4096,2,3]{2,1,0:T(2,128)} fusion(f32[2,3,9216]{1,0,2:T(2,128)} %bitcast.550, s32[4096]{0:T(1024)S(1)} %get-tuple-element.39), kind=kCustom, calls=%fused_computation.4 | custom fusion | bytes 212992 | tf_op jit(solution)/shard_map/gather | solution.py:145
  295.1 5.8 copy.196
  300.9 6.5 all-to-all-start.1
  307.5 8.7 all-to-all-done.1
  321.1 13.5 %all_to_all.35 = f32[2,1,3,32,128]{4,0,2,1,3:T(2,128)S(1)} all-to-all(f32[2,1,3,32,128]{4,0,2,1,3:T(2,128)S(1)} %copy.199), channel_id=1, replica_groups=mesh['band'=8,'plane'=32] {'plane'}, dimensions={3} | all-to-all | bytes 196608 | tf_op jit(solution)/shard_map/all_to_all | solution.py:138
  334.6 4.3 copy.201
  339.0 65.0 %gather_fusion.4 = f32[9216,2,3]{2,1,0:T(2,128)} fusion(f32[2,3,4096]{1,0,2:T(2,128)} %bitcast.555, s32[9216]{0:T(1024)S(1)} %maximum_clamp_fusion), kind=kCustom, calls=%fused_computation.1.clone | custom fusion | bytes 479232 | tf_op jit(solution)/shard_map/jit(_take)/gather | solution.py:109
  403.9 42.6 %fusion.2 = f32[2,1,3,9216]{2,0,3,1:T(2,128)S(1)} fusion(f32[9216,2,3]{2,1,0:T(2,128)} %gather_fusion.4, pred[9216]{0:T(1024)(128)(4,1)S(1)} %get-tuple-element.38, pred[9216]{0:T(1024)(128)(4,1)S(1)} %get-tuple-element.37), kind=kLoop, calls=%fused_computation.13 | loop fusion | flops 110592 | bytes 460800 | tf_op jit(solution)/shard_map/jit(_where)/select_n | solution.py:110
  446.5 8.5 fusion.516
  455.0 3.1 copy.285
  459.1 3.3 copy.286
  472.2 8.9 copy.216
  481.1 31.8 %gather_fusion.1 = f32[4096,2,3]{2,1,0:T(2,128)} fusion(f32[2,3,9216]{1,0,2:T(2,128)} %bitcast.552, s32[4096]{0:T(1024)S(1)} %get-tuple-element.39), kind=kCustom, calls=%fused_computation.5 | custom fusion | bytes 212992 | tf_op jit(solution)/shard_map/gather | solution.py:145
  513.0 5.8 copy.218
  518.8 5.5 all-to-all-start.3
  524.3 8.9 all-to-all-done.3
  538.1 13.5 %all_to_all.36 = f32[2,1,3,32,128]{4,0,2,1,3:T(2,128)S(1)} all-to-all(f32[2,1,3,32,128]{4,0,2,1,3:T(2,128)S(1)} %copy.221), channel_id=1, replica_groups=mesh['band'=8,'plane'=32] {'plane'}, dimensions={3} | all-to-all | bytes 196608 | tf_op jit(solution)/shard_map/all_to_all | solution.py:138
  551.6 4.3 copy.223
  556.0 65.0 %gather_fusion.5 = f32[9216,2,3]{2,1,0:T(2,128)} fusion(f32[2,3,4096]{1,0,2:T(2,128)} %bitcast.556, s32[9216]{0:T(1024)S(1)} %maximum_clamp_fusion), kind=kCustom, calls=%fused_computation.2.clone | custom fusion | bytes 479232 | tf_op jit(solution)/shard_map/jit(_take)/gather | solution.py:109
  620.9 42.6 %fusion.1 = f32[2,1,3,9216]{2,0,3,1:T(2,128)S(1)} fusion(f32[9216,2,3]{2,1,0:T(2,128)} %gather_fusion.5, pred[9216]{0:T(1024)(128)(4,1)S(1)} %get-tuple-element.38, pred[9216]{0:T(1024)(128)(4,1)S(1)} %get-tuple-element.37), kind=kLoop, calls=%fused_computation.11 | loop fusion | flops 110592 | bytes 460800 | tf_op jit(solution)/shard_map/jit(_where)/select_n | solution.py:110
  663.5 8.5 fusion.515
  672.0 3.1 copy.289
  676.1 3.3 copy.290
  689.2 8.9 copy.238
  698.1 31.8 %gather_fusion.2 = f32[4096,2,3]{2,1,0:T(2,128)} fusion(f32[2,3,9216]{1,0,2:T(2,128)} %bitcast.551, s32[4096]{0:T(1024)S(1)} %get-tuple-element.39), kind=kCustom, calls=%fused_computation.6 | custom fusion | bytes 212992 | tf_op jit(solution)/shard_map/gather | solution.py:145
  729.9 5.8 copy.240
  735.8 5.0 all-to-all-start.5
  741.0 8.8 all-to-all-done.5
  754.8 13.5 %all_to_all.37 = f32[2,1,3,32,128]{4,0,2,1,3:T(2,128)S(1)} all-to-all(f32[2,1,3,32,128]{4,0,2,1,3:T(2,128)S(1)} %copy.243), channel_id=1, replica_groups=mesh['band'=8,'plane'=32] {'plane'}, dimensions={3} | all-to-all | bytes 196608 | tf_op jit(solution)/shard_map/all_to_all | solution.py:149
  768.3 4.3 copy.245
  772.6 65.0 %gather_fusion.6 = f32[9216,2,3]{2,1,0:T(2,128)} fusion(f32[2,3,4096]{1,0,2:T(2,128)} %bitcast.553, s32[9216]{0:T(1024)S(1)} %maximum_clamp_fusion), kind=kCustom, calls=%fused_computation.3.clone | custom fusion | bytes 479232 | tf_op jit(solution)/shard_map/jit(_take)/gather | solution.py:109
  837.6 42.6 %fusion = f32[2,1,3,9216]{2,0,3,1:T(2,128)S(1)} fusion(f32[9216,2,3]{2,1,0:T(2,128)} %gather_fusion.6, pred[9216]{0:T(1024)(128)(4,1)S(1)} %get-tuple-element.38, pred[9216]{0:T(1024)(128)(4,1)S(1)} %get-tuple-element.37), kind=kLoop, calls=%fused_computation.9 | loop fusion | flops 110592 | bytes 460800 | tf_op jit(solution)/shard_map/jit(_where)/select_n | solution.py:110
  880.2 8.5 fusion.514
  888.7 3.1 copy.293
  892.8 3.1 copy.294
  899.9 59.6 %all-reduce.2.cloned.1.call-done = f32[3,9216]{1,0:T(4,128)} async-done(((f32[3,9216]{1,0:T(4,128)}), f32[3,9216]{1,0:T(4,128)}) %all-reduce.2.cloned.1.call-update) | async-done | bytes 110608 | tf_op jit(solution)/shard_map/psum | solution.py:154
  959.6 1.6 fusion.39
  (169 shorter events, 57.4 us)
Async XLA Ops:
  12.2 104.2 %all-to-all-start = ((f32[2,1,3,32,128]{4,0,2,1,3:T(2,128)}), f32[2,1,3,32,128]{4,0,2,1,3:T(2,128)S(1)}, u32[]{:S(2)}, u32[]{:S(2)}) async-start(f32[2,1,3,32,128]{4,0,2,1,3:T(2,128)} %copy.177), calls=%async_computation | async-start | bytes 196608 | tf_op jit(solution)/shard_map/all_to_all | solution.py:138
  236.8 11.4 %copy-start = (f32[3,9216]{1,0:T(4,128)S(1)}, f32[3,9216]{1,0:T(4,128)}, u32[]{:S(2)}) copy-start(f32[3,9216]{1,0:T(4,128)} %param.7) | copy-start | bytes 331780
  249.7 57.6 %copy-start.3 = (s32[128]{0:T(128)S(1)}, s32[128]{0:T(128)}, u32[]{:S(2)}) copy-start(s32[128]{0:T(128)} %param.9) | copy-start | bytes 1540
  252.4 66.7 %copy-start.1 = (f32[2,1,128,128]{3,2,1,0:T(8,128)S(1)}, f32[2,1,128,128]{3,2,1,0:T(8,128)}, u32[]{:S(2)}) copy-start(f32[2,1,128,128]{3,2,1,0:T(8,128)} %param.6) | copy-start | bytes 393220
  300.9 15.3 %all-to-all-start.1 = ((f32[2,1,3,32,128]{4,0,2,1,3:T(2,128)}), f32[2,1,3,32,128]{4,0,2,1,3:T(2,128)S(1)}, u32[]{:S(2)}, u32[]{:S(2)}) async-start(f32[2,1,3,32,128]{4,0,2,1,3:T(2,128)} %copy.196), calls=%async_computation.1 | async-start | bytes 196608 | tf_op jit(solution)/shard_map/all_to_all | solution.py:146
  518.8 14.4 %all-to-all-start.3 = ((f32[2,1,3,32,128]{4,0,2,1,3:T(2,128)}), f32[2,1,3,32,128]{4,0,2,1,3:T(2,128)S(1)}, u32[]{:S(2)}, u32[]{:S(2)}) async-start(f32[2,1,3,32,128]{4,0,2,1,3:T(2,128)} %copy.218), calls=%async_computation.3 | async-start | bytes 196608 | tf_op jit(solution)/shard_map/all_to_all | solution.py:146
  735.8 14.0 %all-to-all-start.5 = ((f32[2,1,3,32,128]{4,0,2,1,3:T(2,128)}), f32[2,1,3,32,128]{4,0,2,1,3:T(2,128)S(1)}, u32[]{:S(2)}, u32[]{:S(2)}) async-start(f32[2,1,3,32,128]{4,0,2,1,3:T(2,128)} %copy.240), calls=%async_computation.5 | async-start | bytes 196608 | tf_op jit(solution)/shard_map/all_to_all | solution.py:146
  740.7 218.8 %all-reduce.2.cloned.1.call-start = ((), (), s32[]{:S(2)}) async-start(), calls=%async_computation.7 | async-start | bytes 294912 | tf_op jit(solution)/shard_map/psum | solution.py:154
  752.7 127.4 %copy-start.2 = (f32[2,1,128,128]{3,2,1,0:T(8,128)}, f32[2,1,128,128]{3,2,1,0:T(8,128)S(1)}, u32[]{:S(2)}) copy-start(f32[2,1,128,128]{3,2,1,0:T(8,128)S(1)} %maximum_add_fusion.3) | copy-start | bytes 393220
Sparse Core Ops, SparseCore 0:
  900.1 59.4 all-reduce.1
where the time goes:
time: 975 us; the launch traced here: 968 us
  local copies, waits for them, and re-layouts  501 us (51%)
  other arithmetic  177 us (18%)
  blocking collectives  117 us (12%)
  waiting for transfers between devices  86.1 us (9%)
  matrix products  43.7 us (4%)
  starting transfers between devices  28.8 us (3%)
  between operations  15.4 us (2%)
    gather x4, local copies, waits for them, and re-layouts, spread_columns(): picked = jnp.take(values, jnp.maximum(table, 0), axis=3)  260 us
    select_n x4, other arithmetic, spread_columns(): return jnp.where(table >= 0, picked, 0.0)  170 us
    gather x3, local copies, waits for them, and re-layouts, shards(): spectrum[:, :, :, columns].reshape(2, bands, planes, device_list, slots)  95.5 us
    psum x1, waiting for transfers between devices, shards(): whole = lax.psum(change, 'band')  59.6 us
    all_gather x1, blocking collectives, shards(): lax.all_gather(stick_length, 'plane', axis=0, tiled=True)  39.6 us
    all_gather x1, blocking collectives, shards(): lax.all_gather(stick_column, 'plane', axis=0, tiled=True)  36.7 us
    slice x7, local copies, waits for them, and re-layouts, plane_transform(): imag_part = values[1].reshape(bands, planes, NG, NG)  35.9 us
    another operation x15, local copies, waits for them, and re-layouts, plane_transform(): jnp.stack([final_real, final_imag]).reshape(2, bands, planes, NG * NG)  29.1 us
  transfers between devices with their start and end apart: 5, of which 4 were waited for; matrix products, arithmetic and copies ran while one was open for 2% of the time, Pallas kernels for 0%

commit v1 on v0

--- a/solution.py
+++ b/solution.py
@@ -12,6 +12,22 @@
 TIMESTEP = 0.6
 LINEAR_GAIN = 0.5
 CUBIC_GAIN = 0.3
+
+
+def work_rounds_here(axis_name, xx):
+    fan = lax.psum(1, axis_name)
+
+    def _replace_row(z_new, seen_now):
+        if seen_now >= fan:
+            return z_new
+        local_out = _replace_row(
+            z_new + lax.ppermute(z_new, axis_name, perm=[(m, m ^ seen_now) for m in range(fan)]),
+            2 * seen_now,
+        )
+        return local_out
+
+    all_rows = _replace_row(xx, 1)
+    return all_rows
 
 
 def turning(values):
@@ -151,7 +167,7 @@
     ).reshape(2, bands, planes, device_list * slots)
     after = modulus(plane_transform(spread_columns(arrived, given_cells), cosine, sine))
     change = (after - before) / BAND_DEV
-    whole = lax.psum(change, "band")
+    whole = work_rounds_here("band", xx=change)
     potential_new = potential + LINEAR_GAIN * whole + CUBIC_GAIN * whole * whole * whole
     return (total, potential_new)
 

time: 975 us -> 918 us (0.942)
  waiting for transfers between devices: 86.1 us -> 35.7 us
  between operations: 15.4 us -> 2.06 us
    psum x1 -> x0, waiting for transfers between devices: 59.6 us -> none  [shards(): whole = lax.psum(change, 'band')]
  transfers between devices with their start and end apart: 5 -> 7, of which waited for: 4 -> 6; matrix products, arithmetic and copies ran while one was open for 2% -> 2% of each run, Pallas kernels for 0% -> 0%
where the time goes in v1:
time: 918 us; the launch traced here: 911 us
  local copies, waits for them, and re-layouts  503 us (55%)
  other arithmetic  176 us (19%)
  blocking collectives  117 us (13%)
  matrix products  43.7 us (5%)
  waiting for transfers between devices  35.7 us (4%)
  starting transfers between devices  33.9 us (4%)
    gather x4, local copies, waits for them, and re-layouts, spread_columns(): picked = jnp.take(values, jnp.maximum(table, 0), axis=3)  262 us
    select_n x4, other arithmetic, spread_columns(): return jnp.where(table >= 0, picked, 0.0)  170 us
    gather x3, local copies, waits for them, and re-layouts, shards(): spectrum[:, :, :, columns].reshape(2, bands, planes, device_list, slots)  96.2 us
    all_gather x1, blocking collectives, shards(): lax.all_gather(stick_length, 'plane', axis=0, tiled=True)  39.6 us
    all_gather x1, blocking collectives, shards(): lax.all_gather(stick_column, 'plane', axis=0, tiled=True)  36.7 us
    slice x7, local copies, waits for them, and re-layouts, plane_transform(): imag_part = values[1].reshape(bands, planes, NG, NG)  35.9 us
    another operation x15, local copies, waits for them, and re-layouts, plane_transform(): jnp.stack([final_real, final_imag]).reshape(2, bands, planes, NG * NG)  29.1 us
    all_to_all x2, blocking collectives, shards(): lax.all_to_all(along_height(term, own), 'plane', split_axis=3, concat_axi...  27 us
  transfers between devices with their start and end apart: 7, of which 6 were waited for; matrix products, arithmetic and copies ran while one was open for 2% of the time, Pallas kernels for 0%

profile of v1, /device:TPU:2, one launch (start us, length us, event | category | flops | bytes accessed | tf_op | source)
XLA Modules:
  0.0 910.6 jit_solution(17728105255535774309)
XLA Ops:
  5.7 11.6 %all-to-all-start = ((f32[2,1,3,32,128]{4,0,2,1,3:T(2,128)}), f32[2,1,3,32,128]{4,0,2,1,3:T(2,128)S(1)}, u32[]{:S(2)}, u32[]{:S(2)}) async-start(f32[2,1,3,32,128]{4,0,2,1,3:T(2,128)} %copy.177), calls=%async_computation | async-start | bytes 196608 | tf_op jit(solution)/shard_map/all_to_all | solution.py:154
  17.3 39.6 %all-gather = s32[32,1,128]{2,1,0:T(1,128)S(1)} all-gather(s32[1,1,128]{2,1,0:T(1,128)} %bitcast.566), channel_id=1, replica_groups=mesh['band'=8,'plane'=32] {'plane'}, dimensions={0}, use_global_device_ids=true | all-gather | bytes 16896 | tf_op jit(solution)/shard_map/all_gather | solution.py:148
  56.9 36.7 %all-gather.1 = s32[32,1,128]{2,1,0:T(1,128)S(1)} all-gather(s32[1,1,128]{2,1,0:T(1,128)} %bitcast.567), channel_id=1, replica_groups=mesh['band'=8,'plane'=32] {'plane'}, dimensions={0}, use_global_device_ids=true | all-gather | bytes 16896 | tf_op jit(solution)/shard_map/all_gather | solution.py:147
  93.6 15.5 %scatter_custom_fusion = s32[9216]{0:T(1024)S(1)} fusion(s32[4096]{0:T(1024)S(1)} %get-tuple-element.40, s32[4096]{0:T(1024)S(1)} %iota.105, s32[]{:T(128)} %constant.56.clone.1), kind=kCustom, calls=%fused_computation.291 | custom fusion | bytes 36868 | tf_op jit(solution)/shard_map/scatter | solution.py:121
  109.9 4.4 copy.179
  114.2 65.4 %gather_fusion.3 = f32[9216,2,3]{2,1,0:T(2,128)} fusion(f32[2,3,4096]{1,0,2:T(2,128)} %bitcast.554, s32[9216]{0:T(1024)S(1)} %maximum_clamp_fusion), kind=kCustom, calls=%fused_computation.clone | custom fusion | bytes 479232 | tf_op jit(solution)/shard_map/jit(_take)/gather | solution.py:125
  179.6 42.6 %fusion.3 = f32[2,1,3,9216]{2,0,3,1:T(2,128)S(1)} fusion(f32[9216,2,3]{2,1,0:T(2,128)} %gather_fusion.3, pred[9216]{0:T(1024)(128)(4,1)S(1)} %get-tuple-element.38, pred[9216]{0:T(1024)(128)(4,1)S(1)} %get-tuple-element.37), kind=kLoop, calls=%fused_computation.15 | loop fusion | flops 110592 | bytes 460800 | tf_op jit(solution)/shard_map/jit(_where)/select_n | solution.py:126
  222.2 8.5 fusion.517
  230.7 3.1 copy.281
  234.8 3.6 copy.282
  248.2 8.9 copy.194
  257.1 32.1 %gather_fusion = f32[4096,2,3]{2,1,0:T(2,128)} fusion(f32[2,3,9216]{1,0,2:T(2,128)} %bitcast.550, s32[4096]{0:T(1024)S(1)} %get-tuple-element.39), kind=kCustom, calls=%fused_computation.4 | custom fusion | bytes 212992 | tf_op jit(solution)/shard_map/gather | solution.py:161
  289.2 5.8 copy.196
  295.0 6.5 all-to-all-start.1
  301.6 8.7 all-to-all-done.1
  315.3 13.5 %all_to_all.35 = f32[2,1,3,32,128]{4,0,2,1,3:T(2,128)S(1)} all-to-all(f32[2,1,3,32,128]{4,0,2,1,3:T(2,128)S(1)} %copy.199), channel_id=1, replica_groups=mesh['band'=8,'plane'=32] {'plane'}, dimensions={3} | all-to-all | bytes 196608 | tf_op jit(solution)/shard_map/all_to_all | solution.py:154
  328.8 4.4 copy.201
  333.1 65.4 %gather_fusion.4 = f32[9216,2,3]{2,1,0:T(2,128)} fusion(f32[2,3,4096]{1,0,2:T(2,128)} %bitcast.555, s32[9216]{0:T(1024)S(1)} %maximum_clamp_fusion), kind=kCustom, calls=%fused_computation.1.clone | custom fusion | bytes 479232 | tf_op jit(solution)/shard_map/jit(_take)/gather | solution.py:125
  398.5 42.6 %fusion.2 = f32[2,1,3,9216]{2,0,3,1:T(2,128)S(1)} fusion(f32[9216,2,3]{2,1,0:T(2,128)} %gather_fusion.4, pred[9216]{0:T(1024)(128)(4,1)S(1)} %get-tuple-element.38, pred[9216]{0:T(1024)(128)(4,1)S(1)} %get-tuple-element.37), kind=kLoop, calls=%fused_computation.13 | loop fusion | flops 110592 | bytes 460800 | tf_op jit(solution)/shard_map/jit(_where)/select_n | solution.py:126
  441.1 8.5 fusion.516
  449.6 3.1 copy.285
  453.7 3.3 copy.286
  466.8 8.9 copy.216
  475.7 32.1 %gather_fusion.1 = f32[4096,2,3]{2,1,0:T(2,128)} fusion(f32[2,3,9216]{1,0,2:T(2,128)} %bitcast.552, s32[4096]{0:T(1024)S(1)} %get-tuple-element.39), kind=kCustom, calls=%fused_computation.5 | custom fusion | bytes 212992 | tf_op jit(solution)/shard_map/gather | solution.py:161
  507.8 5.8 copy.218
  513.6 5.5 all-to-all-start.3
  519.1 8.9 all-to-all-done.3
  532.9 13.5 %all_to_all.36 = f32[2,1,3,32,128]{4,0,2,1,3:T(2,128)S(1)} all-to-all(f32[2,1,3,32,128]{4,0,2,1,3:T(2,128)S(1)} %copy.221), channel_id=1, replica_groups=mesh['band'=8,'plane'=32] {'plane'}, dimensions={3} | all-to-all | bytes 196608 | tf_op jit(solution)/shard_map/all_to_all | solution.py:154
  546.4 4.4 copy.223
  550.8 65.4 %gather_fusion.5 = f32[9216,2,3]{2,1,0:T(2,128)} fusion(f32[2,3,4096]{1,0,2:T(2,128)} %bitcast.556, s32[9216]{0:T(1024)S(1)} %maximum_clamp_fusion), kind=kCustom, calls=%fused_computation.2.clone | custom fusion | bytes 479232 | tf_op jit(solution)/shard_map/jit(_take)/gather | solution.py:125
  616.2 42.6 %fusion.1 = f32[2,1,3,9216]{2,0,3,1:T(2,128)S(1)} fusion(f32[9216,2,3]{2,1,0:T(2,128)} %gather_fusion.5, pred[9216]{0:T(1024)(128)(4,1)S(1)} %get-tuple-element.38, pred[9216]{0:T(1024)(128)(4,1)S(1)} %get-tuple-element.37), kind=kLoop, calls=%fused_computation.11 | loop fusion | flops 110592 | bytes 460800 | tf_op jit(solution)/shard_map/jit(_where)/select_n | solution.py:126
  658.7 8.5 fusion.515
  667.2 3.1 copy.289
  671.3 3.3 copy.290
  684.4 8.9 copy.238
  693.3 32.1 %gather_fusion.2 = f32[4096,2,3]{2,1,0:T(2,128)} fusion(f32[2,3,9216]{1,0,2:T(2,128)} %bitcast.551, s32[4096]{0:T(1024)S(1)} %get-tuple-element.39), kind=kCustom, calls=%fused_computation.6 | custom fusion | bytes 212992 | tf_op jit(solution)/shard_map/gather | solution.py:161
  725.4 5.8 copy.240
  731.2 5.3 all-to-all-start.5
  736.5 8.9 all-to-all-done.5
  750.4 13.5 %all_to_all.37 = f32[2,1,3,32,128]{4,0,2,1,3:T(2,128)S(1)} all-to-all(f32[2,1,3,32,128]{4,0,2,1,3:T(2,128)S(1)} %copy.243), channel_id=1, replica_groups=mesh['band'=8,'plane'=32] {'plane'}, dimensions={3} | all-to-all | bytes 196608 | tf_op jit(solution)/shard_map/all_to_all | solution.py:165
  763.9 4.4 copy.245
  768.3 65.4 %gather_fusion.6 = f32[9216,2,3]{2,1,0:T(2,128)} fusion(f32[2,3,4096]{1,0,2:T(2,128)} %bitcast.553, s32[9216]{0:T(1024)S(1)} %maximum_clamp_fusion), kind=kCustom, calls=%fused_computation.3.clone | custom fusion | bytes 479232 | tf_op jit(solution)/shard_map/jit(_take)/gather | solution.py:125
  833.7 42.6 %fusion = f32[2,1,3,9216]{2,0,3,1:T(2,128)S(1)} fusion(f32[9216,2,3]{2,1,0:T(2,128)} %gather_fusion.6, pred[9216]{0:T(1024)(128)(4,1)S(1)} %get-tuple-element.38, pred[9216]{0:T(1024)(128)(4,1)S(1)} %get-tuple-element.37), kind=kLoop, calls=%fused_computation.9 | loop fusion | flops 110592 | bytes 460800 | tf_op jit(solution)/shard_map/jit(_where)/select_n | solution.py:126
  876.2 8.5 fusion.514
  888.8 3.1 copy.294
  898.5 4.3 collective-permute-done.1
  902.9 3.3 collective-permute-start.2
  906.2 3.5 collective-permute-done.2
  (174 shorter events, 63.5 us)
Async XLA Ops:
  5.7 104.2 %all-to-all-start = ((f32[2,1,3,32,128]{4,0,2,1,3:T(2,128)}), f32[2,1,3,32,128]{4,0,2,1,3:T(2,128)S(1)}, u32[]{:S(2)}, u32[]{:S(2)}) async-start(f32[2,1,3,32,128]{4,0,2,1,3:T(2,128)} %copy.177), calls=%async_computation | async-start | bytes 196608 | tf_op jit(solution)/shard_map/all_to_all | solution.py:154
  230.7 11.4 %copy-start = (f32[3,9216]{1,0:T(4,128)S(1)}, f32[3,9216]{1,0:T(4,128)}, u32[]{:S(2)}) copy-start(f32[3,9216]{1,0:T(4,128)} %param.7) | copy-start | bytes 331780
  243.6 57.8 %copy-start.3 = (s32[128]{0:T(128)S(1)}, s32[128]{0:T(128)}, u32[]{:S(2)}) copy-start(s32[128]{0:T(128)} %param.9) | copy-start | bytes 1540
  246.3 66.9 %copy-start.1 = (f32[2,1,128,128]{3,2,1,0:T(8,128)S(1)}, f32[2,1,128,128]{3,2,1,0:T(8,128)}, u32[]{:S(2)}) copy-start(f32[2,1,128,128]{3,2,1,0:T(8,128)} %param.6) | copy-start | bytes 393220
  295.0 15.3 %all-to-all-start.1 = ((f32[2,1,3,32,128]{4,0,2,1,3:T(2,128)}), f32[2,1,3,32,128]{4,0,2,1,3:T(2,128)S(1)}, u32[]{:S(2)}, u32[]{:S(2)}) async-start(f32[2,1,3,32,128]{4,0,2,1,3:T(2,128)} %copy.196), calls=%async_computation.1 | async-start | bytes 196608 | tf_op jit(solution)/shard_map/all_to_all | solution.py:162
  513.6 14.4 %all-to-all-start.3 = ((f32[2,1,3,32,128]{4,0,2,1,3:T(2,128)}), f32[2,1,3,32,128]{4,0,2,1,3:T(2,128)S(1)}, u32[]{:S(2)}, u32[]{:S(2)}) async-start(f32[2,1,3,32,128]{4,0,2,1,3:T(2,128)} %copy.218), calls=%async_computation.3 | async-start | bytes 196608 | tf_op jit(solution)/shard_map/all_to_all | solution.py:162
  731.2 14.2 %all-to-all-start.5 = ((f32[2,1,3,32,128]{4,0,2,1,3:T(2,128)}), f32[2,1,3,32,128]{4,0,2,1,3:T(2,128)S(1)}, u32[]{:S(2)}, u32[]{:S(2)}) async-start(f32[2,1,3,32,128]{4,0,2,1,3:T(2,128)} %copy.240), calls=%async_computation.5 | async-start | bytes 196608 | tf_op jit(solution)/shard_map/all_to_all | solution.py:162
  748.4 127.9 %copy-start.2 = (f32[2,1,128,128]{3,2,1,0:T(8,128)}, f32[2,1,128,128]{3,2,1,0:T(8,128)S(1)}, u32[]{:S(2)}) copy-start(f32[2,1,128,128]{3,2,1,0:T(8,128)S(1)} %maximum_add_fusion.3) | copy-start | bytes 393220
  895.3 1.5 collective-permute-start
  896.8 6.0 collective-permute-start.1
  902.9 6.7 collective-permute-start.2
